TPU v7x, 32 devices: a whole 2x2x4 slice. The times are simulated.
32 devices in a mesh: row: 8 (over z, y), col: 4 (over x, core).
Axes of the slice: x: 2, y: 2, z: 4, core: 2. Of those that a mesh axis runs over, the one named last changes fastest.
Arguments:
- start_block: float32 [64, 16, 128], P(('row', 'col')), may hold values from -6 to 6
- blocks: float32 [8, 4, 58, 128, 128], P('row', 'col'), as said below
- slot_row: int32 [8, 4, 58], P('row', 'col'), may hold values from 0 to 7, as said below
- slot_col: int32 [8, 4, 58], P('row', 'col'), may hold values from 0 to 15, as said below
- counts: int32 [8, 4], P('row', 'col'), may hold values from 34 to 58, as said below
Outputs:
- alphas: float32 [2, 16, 16], replicated
- betas: float32 [2, 16, 16], replicated
- next_block: float32 [64, 16, 128], P(('row', 'col'))
Inputs may be any that keep to these rules, and one draw needn't show every extreme that they name: `blocks`: over all cells the live slots list each nonzero block of a symmetric matrix exactly once: block (J, I) is listed exactly when (I, J) is, holding its transpose. Slots at or past a cell's count hold finite values that are no part of H. `counts`: live slots of a cell come first; in every draw some cell has all 58 slots live. `slot_row`: for live slots, the block row within the cell's row group of 8 block rows. `slot_col`: for live slots, the position within the cell's column group of 16 block columns, as in the first step.
All inputs are finite; a program needn't handle non-finite values.
Results may differ from a plain program's by a relative error of at most 0.0003.
Values sent between devices are 32-bit elements; how exact they have to be, the bound alone decides.
A program may use at most 64 MiB of HBM per device.

v0:
```python
import jax
import jax.numpy as jnp
from jax import lax
from jax.sharding import PartitionSpec as P

ITERS = 2
highest = lax.Precision.HIGHEST


def matmul(left, right):
    return jnp.dot(left, right, precision=highest, preferred_element_type=jnp.float32)


def local_gram(left, right):
    return jnp.einsum(
        "bki,bli->kl", left, right, precision=highest, preferred_element_type=jnp.float32
    )


def on_device(start_block, blocks, slot_row, slot_col, counts):
    matrix_tiles = blocks[0, 0]
    rows_local = slot_row[0, 0]
    cols_local = slot_col[0, 0]
    capacity = matrix_tiles.shape[0]
    active = lax.iota(jnp.int32, capacity) < counts[0, 0]
    piece_rows = start_block.shape[0]
    vec_count = start_block.shape[1]
    orbitals = start_block.shape[2]
    row_total = float(piece_rows * lax.axis_size("row") * lax.axis_size("col") * orbitals)
    identity = jnp.eye(vec_count, dtype=jnp.float32)
    start_mean = lax.psum(local_gram(start_block, start_block), ("row", "col")) / row_total
    factor = jnp.linalg.cholesky(start_mean)
    inverse = jax.scipy.linalg.solve_triangular(factor, identity, lower=True)
    vectors = jnp.einsum(
        "kl,bli->bki", inverse, start_block, precision=highest, preferred_element_type=jnp.float32
    )
    previous = jnp.zeros(vectors.shape, jnp.float32)
    beta_prev = jnp.zeros((vec_count, vec_count), jnp.float32)
    alpha_list = []
    beta_list = []
    for iteration in range(ITERS):
        gathered = lax.all_gather(vectors, "row", axis=0, tiled=True)
        operate_product = jnp.einsum(
            "sij,skj->ski",
            matrix_tiles,
            gathered[cols_local],
            precision=highest,
            preferred_element_type=jnp.float32,
        )
        targets = lax.iota(jnp.int32, lax.axis_size("col") * piece_rows)
        selector = ((rows_local[None, :] == targets[:, None]) & active[None, :]).astype(jnp.float32)
        image_block = lax.psum_scatter(
            jnp.einsum(
                "rs,ski->rki",
                selector,
                operate_product,
                precision=highest,
                preferred_element_type=jnp.float32,
            ),
            "col",
            scatter_dimension=0,
            tiled=True,
        )
        stacked = jnp.concatenate([image_block, vectors, previous], axis=1)
        all_means = lax.psum(local_gram(stacked, stacked), ("row", "col")) / row_total
        yy_mean = all_means[:vec_count, :vec_count]
        vy_mean = all_means[vec_count : 2 * vec_count, :vec_count]
        py_mean = all_means[2 * vec_count :, :vec_count]
        vv_mean = all_means[vec_count : 2 * vec_count, vec_count : 2 * vec_count]
        pv_mean = all_means[2 * vec_count :, vec_count : 2 * vec_count]
        pp_mean = all_means[2 * vec_count :, 2 * vec_count :]
        residual = image_block - jnp.einsum(
            "lk,bli->bki", vy_mean, vectors, precision=highest, preferred_element_type=jnp.float32
        )
        residual = residual - jnp.einsum(
            "kl,bli->bki",
            beta_prev,
            previous,
            precision=highest,
            preferred_element_type=jnp.float32,
        )
        gram_mean = yy_mean - matmul(vy_mean.T, vy_mean) - matmul(vy_mean.T, vy_mean)
        gram_mean = gram_mean + matmul(matmul(vy_mean.T, vv_mean), vy_mean)
        gram_mean = gram_mean - matmul(py_mean.T, beta_prev.T) - matmul(beta_prev, py_mean)
        gram_mean = gram_mean + matmul(matmul(vy_mean.T, pv_mean.T), beta_prev.T)
        gram_mean = gram_mean + matmul(matmul(beta_prev, pv_mean), vy_mean)
        gram_mean = gram_mean + matmul(matmul(beta_prev, pp_mean), beta_prev.T)
        factor = jnp.linalg.cholesky(gram_mean)
        beta_block = factor.T
        inverse = jax.scipy.linalg.solve_triangular(factor, identity, lower=True)
        previous = vectors
        vectors = jnp.einsum(
            "kl,bli->bki", inverse, residual, precision=highest, preferred_element_type=jnp.float32
        )
        beta_prev = beta_block
        alpha_list.append(vy_mean)
        beta_list.append(beta_block)
    return (jnp.stack(alpha_list), jnp.stack(beta_list), vectors)


def solution(mesh):
    placed = (
        P(("row", "col"), None, None),
        P("row", "col", None, None, None),
        P("row", "col", None),
        P("row", "col", None),
        P("row", "col"),
    )
    return jax.shard_map(
        on_device,
        mesh=mesh,
        in_specs=placed,
        out_specs=(P(), P(), P(("row", "col"), None, None)),
        check_vma=False,
    )
```

profile of v0, /device:TPU:0, one launch (start us, length us, event | category | flops | bytes accessed | tf_op | source)
XLA Modules:
  0.0 285.7 jit_solution(17474431526224107313)
XLA Ops:
  7.9 0.7 fusion.84
  8.6 0.1 convolution_bitcast_fusion.12
  8.7 42.0 %psum.21 = f32[16,16]{0,1:T(8,128)S(1)} all-reduce(f32[16,16]{0,1:T(8,128)S(1)} %convolution_bitcast_fusion.12), channel_id=1, replica_groups=mesh['row'=8,'col'=4] {'row','col'}, use_global_device_ids=true, to_apply=%region_0.0 | all-reduce | flops 256 | bytes 2048 | tf_op jit(solution)/shard_map/psum | solution.py:31
  50.8 1.5 cholesky.59
  52.3 0.6 compare_reduce_fusion.2
  52.9 0.6 fusion.25
  53.6 1.2 custom-call.7
  54.8 0.2 convolution_bitcast_fusion.11
  55.0 0.1 convolution_bitcast_fusion.8
  55.1 30.6 %all_gather.6 = f32[16,16,128]{2,1,0:T(8,128)S(1)} all-gather(f32[2,16,128]{2,1,0:T(8,128)S(1)} %convolution_bitcast_fusion.8), channel_id=1, replica_groups=mesh['row'=8,'col'=4] {'row'}, dimensions={0}, use_global_device_ids=true | all-gather | bytes 147456 | tf_op jit(solution)/shard_map/all_gather | solution.py:42
  85.7 0.6 gather_fusion
  86.4 8.1 %fusion.2 = f32[58,16,128]{2,1,0:T(8,128)S(1)} fusion(f32[58,16,128]{2,1,0:T(8,128)S(1)} %gather_fusion, f32[1,1,58,128,128]{4,3,2,1,0:T(8,128)} %param.9), kind=kOutput, calls=%fused_computation.4 | convolution fusion | flops 182452224 | bytes 4751360 | tf_op jit(solution)/shard_map/sij,skj->ski/dot_general | solution.py:43
  94.4 0.4 fusion.10
  94.8 0.6 copy.36
  95.6 19.3 %reduce-scatter.3.cloned.1.call-done = f32[2,16,128]{2,1,0:T(8,128)} async-done(((f32[8,16,128]{2,1,0:T(8,128)}), f32[2,16,128]{2,1,0:T(8,128)}) %reduce-scatter.3.cloned.1.call-update) | async-done | bytes 16400 | tf_op jit(solution)/shard_map/reduce_scatter | solution.py:52
  114.9 1.0 convolution_bitcast_fusion.1
  115.9 39.5 %psum.22 = f32[48,48]{0,1:T(8,128)S(1)} all-reduce(f32[48,48]{0,1:T(8,128)S(1)} %convolution_bitcast_fusion.1), channel_id=1, replica_groups=mesh['row'=8,'col'=4] {'row','col'}, use_global_device_ids=true, to_apply=%region_4.0 | all-reduce | flops 2304 | bytes 18432 | tf_op jit(solution)/shard_map/psum | solution.py:65
  155.4 0.2 fusion.50
  155.6 0.2 fusion.30
  155.8 0.2 fusion.52
  156.0 0.2 fusion.32
  156.2 0.2 subtract_subtract_fusion.1
  156.4 0.9 fusion.7
  157.5 0.2 convolution_add_fusion.7
  157.7 0.2 convolution_subtract_fusion.3
  157.9 0.2 convolution_subtract_fusion.2
  158.1 0.1 convolution_add_fusion.6
  158.2 0.2 convolution_add_fusion.5
  158.4 0.1 convolution_add_fusion.4
  158.7 1.5 cholesky.70
  160.2 0.6 compare_reduce_fusion.1
  160.8 0.6 fusion.94
  161.5 1.2 custom-call.8
  162.7 0.2 convolution_bitcast_fusion.10
  162.9 0.1 convolution_bitcast_fusion.5
  163.0 30.7 %all_gather.7 = f32[16,16,128]{2,1,0:T(8,128)S(1)} all-gather(f32[2,16,128]{2,1,0:T(8,128)S(1)} %convolution_bitcast_fusion.5), channel_id=1, replica_groups=mesh['row'=8,'col'=4] {'row'}, dimensions={0}, use_global_device_ids=true | all-gather | bytes 147456 | tf_op jit(solution)/shard_map/all_gather | solution.py:42
  193.8 0.6 gather_fusion.1
  194.4 8.1 %fusion = f32[58,16,128]{2,1,0:T(8,128)S(1)} fusion(f32[58,16,128]{2,1,0:T(8,128)S(1)} %gather_fusion.1, f32[1,1,58,128,128]{4,3,2,1,0:T(8,128)} %param.9), kind=kOutput, calls=%fused_computation.2 | convolution fusion | flops 182452224 | bytes 4751360 | tf_op jit(solution)/shard_map/sij,skj->ski/dot_general | solution.py:43
  202.5 0.4 fusion.8
  202.9 0.6 copy.47
  203.6 20.4 %reduce-scatter.5.cloned.1.call-done = f32[2,16,128]{2,1,0:T(8,128)} async-done(((f32[8,16,128]{2,1,0:T(8,128)}), f32[2,16,128]{2,1,0:T(8,128)}) %reduce-scatter.5.cloned.1.call-update) | async-done | bytes 16400 | tf_op jit(solution)/shard_map/reduce_scatter | solution.py:52
  223.9 1.0 convolution_bitcast_fusion
  224.9 39.5 %psum.23 = f32[48,48]{0,1:T(8,128)S(1)} all-reduce(f32[48,48]{0,1:T(8,128)S(1)} %convolution_bitcast_fusion), channel_id=1, replica_groups=mesh['row'=8,'col'=4] {'row','col'}, use_global_device_ids=true, to_apply=%region_6.9 | all-reduce | flops 2304 | bytes 18432 | tf_op jit(solution)/shard_map/psum | solution.py:65
  264.4 0.8 fusion.44
  265.3 0.9 fusion.26
  266.1 0.2 fusion.46
  266.4 0.2 fusion.28
  266.6 0.2 subtract_subtract_fusion
  266.9 0.9 fusion.5
  267.8 0.8 fusion.4
  268.6 0.2 convolution_add_fusion.3
  268.8 0.9 convolution_subtract_fusion.1
  269.7 0.9 convolution_subtract_fusion
  270.6 0.7 copy.58
  271.2 0.8 convolution_add_fusion.2
  272.1 0.2 convolution_add_fusion.1
  272.3 0.9 convolution_add_fusion
  273.2 1.5 cholesky.81
  274.7 0.6 compare_reduce_fusion
  275.4 0.6 select_bitcast_fusion
  276.0 1.2 custom-call.9
  277.2 0.2 convolution_bitcast_fusion.9
  277.5 0.7 copy.59
  278.2 0.7 convolution_bitcast_fusion.2
  (28 shorter events, 0.8 us)
Async XLA Ops:
  7.2 1.4 copy-start
  7.2 87.3 %copy-start.1 = (s32[1,1,58]{2,1,0:T(1,128)S(1)}, s32[1,1,58]{2,1,0:T(1,128)}, u32[]{:S(2)}) copy-start(s32[1,1,58]{2,1,0:T(1,128)} %param.10) | copy-start | bytes 700
  7.2 107.7 %reduce-scatter.3.cloned.1.call-start = ((), (), s32[]{:S(2)}) async-start(), calls=%async_computation.2 | async-start | bytes 81920 | tf_op jit(solution)/shard_map/reduce_scatter | solution.py:52
  95.5 128.4 %reduce-scatter.5.cloned.1.call-start = ((), (), s32[]{:S(2)}) async-start(), calls=%async_computation.3 | async-start | bytes 81920 | tf_op jit(solution)/shard_map/reduce_scatter | solution.py:52
Sparse Core Ops, SparseCore 0:
  95.6 19.2 reduce-scatter.2
  203.6 20.2 reduce-scatter.4
where the time goes:
time: 287 us; the launch traced here: 286 us
  blocking collectives  182 us (63%)
  waiting for transfers between devices  39.7 us (14%)
  matrix products  31.8 us (11%)
  between operations  14.8 us (5%)
  other arithmetic  12.8 us (4%)
  local copies, waits for them, and re-layouts  4.25 us (1%)
    psum x2, blocking collectives, on_device(): lax.psum(local_gram(stacked, stacked), ('row', 'col')) / row_total  79 us
    all_gather x2, blocking collectives, on_device(): gathered = lax.all_gather(vectors, 'row', axis=0, tiled=True)  61.3 us
    psum x1, blocking collectives, on_device(): lax.psum(local_gram(start_block, start_block), ('row', 'col')) / row_total  42 us
    reduce_scatter x2, waiting for transfers between devices, on_device(): lax.psum_scatter(jnp.einsum('rs,ski->rki', selector, operate_product, pre...  39.7 us
    dot_general x2, matrix products, on_device(): jnp.einsum('sij,skj->ski', matrix_tiles, gathered[cols_local], precision=...  16.1 us
    dot_general x22, matrix products, matmul(): jnp.dot(left, right, precision=highest, preferred_element_type=jnp.float32)  8.28 us
  transfers between devices with their start and end apart: 2, of which 2 were waited for; matrix products, arithmetic and copies ran while one was open for 0% of the time, Pallas kernels for 0%

commit v1 on v0

--- a/solution.py
+++ b/solution.py
@@ -5,6 +5,18 @@
 
 ITERS = 2
 highest = lax.Precision.HIGHEST
+
+
+def ring_gather(shard, axis, dim):
+    ways, here, step = (lax.axis_size(axis), lax.axis_index(axis), shard.shape[dim])
+    shape = [n * ways if d == dim else n for d, n in enumerate(shard.shape)]
+    full = lax.dynamic_update_slice_in_dim(
+        jnp.zeros(shape, shard.dtype), shard, here * step, axis=dim
+    )
+    for far in range(1, ways):
+        shard = lax.ppermute(shard, axis, [(d, (d + 1) % ways) for d in range(ways)])
+        full = lax.dynamic_update_slice_in_dim(full, shard, (here - far) % ways * step, axis=dim)
+    return full
 
 
 def matmul(left, right):
@@ -39,7 +51,7 @@
     alpha_list = []
     beta_list = []
     for iteration in range(ITERS):
-        gathered = lax.all_gather(vectors, "row", axis=0, tiled=True)
+        gathered = ring_gather(vectors, "row", 0)
         operate_product = jnp.einsum(
             "sij,skj->ski",
             matrix_tiles,

time: 287 us -> 311 us (1.084)
  waiting for transfers between devices: 39.7 us -> 120 us
  blocking collectives: 182 us -> 121 us
  starting transfers between devices: 0.08 us -> 4.74 us
    ppermute x0 -> x14, waiting for transfers between devices: none -> 84.2 us  [ring_gather(): lax.ppermute(shard, axis, [(d, (d + 1) % ways) for d in range(ways)])]
    all_gather x2 -> x0, blocking collectives: 61.3 us -> none  [on_device(): gathered = lax.all_gather(vectors, 'row', axis=0, tiled=True)]
    ppermute x0 -> x14, starting transfers between devices: none -> 4.66 us  [ring_gather(): lax.ppermute(shard, axis, [(d, (d + 1) % ways) for d in range(ways)])]
    reduce_scatter x2, waiting for transfers between devices: 39.7 us -> 35.3 us  [on_device(): lax.psum_scatter(jnp.einsum('rs,ski->rki', selector, operate_product, pre...]
  transfers between devices with their start and end apart: 2 -> 16, of which waited for: 2 -> 16; matrix products, arithmetic and copies ran while one was open for 0% -> 0% of each run, Pallas kernels for 0% -> 0%
where the time goes in v1:
time: 311 us; the launch traced here: 310 us
  blocking collectives  121 us (39%)
  waiting for transfers between devices  120 us (39%)
  matrix products  31.8 us (10%)
  between operations  15 us (5%)
  other arithmetic  12.8 us (4%)
  local copies, waits for them, and re-layouts  4.97 us (2%)
  starting transfers between devices  4.74 us (2%)
    ppermute x14, waiting for transfers between devices, ring_gather(): lax.ppermute(shard, axis, [(d, (d + 1) % ways) for d in range(ways)])  84.2 us
    psum x2, blocking collectives, on_device(): lax.psum(local_gram(stacked, stacked), ('row', 'col')) / row_total  79 us
    psum x1, blocking collectives, on_device(): lax.psum(local_gram(start_block, start_block), ('row', 'col')) / row_total  42 us
    reduce_scatter x2, waiting for transfers between devices, on_device(): lax.psum_scatter(jnp.einsum('rs,ski->rki', selector, operate_product, pre...  35.3 us
    dot_general x2, matrix products, on_device(): jnp.einsum('sij,skj->ski', matrix_tiles, gathered[cols_local], precision=...  16.1 us
    dot_general x22, matrix products, matmul(): jnp.dot(left, right, precision=highest, preferred_element_type=jnp.float32)  8.29 us
  transfers between devices with their start and end apart: 16, of which 16 were waited for; matrix products, arithmetic and copies ran while one was open for 0% of the time, Pallas kernels for 0%

profile of v1, /device:TPU:0, one launch (start us, length us, event | category | flops | bytes accessed | tf_op | source)
XLA Modules:
  0.0 309.8 jit_solution(12107275402540058592)
XLA Ops:
  7.2 0.6 copy-done
  8.0 42.0 %psum.21 = f32[16,16]{0,1:T(8,128)S(1)} all-reduce(f32[16,16]{0,1:T(8,128)S(1)} %convolution_bitcast_fusion.12), channel_id=1, replica_groups=mesh['row'=8,'col'=4] {'row','col'}, use_global_device_ids=true, to_apply=%region_0.0 | all-reduce | flops 256 | bytes 2048 | tf_op jit(solution)/shard_map/psum | solution.py:43
  50.1 1.5 cholesky.59
  51.6 0.6 compare_reduce_fusion.2
  52.2 0.6 fusion.25
  52.9 1.2 custom-call.7
  54.5 2.3 collective-permute-start
  56.8 0.7 fusion.84
  58.3 2.7 collective-permute-done
  60.9 6.4 %collective-permute-done.1 = f32[2,16,128]{2,1,0:T(8,128)S(1)} collective-permute-done((f32[2,16,128]{2,1,0:T(8,128)S(1)}, f32[2,16,128]{2,1,0:T(8,128)S(1)}, u32[]{:S(2)}, u32[]{:S(2)}) %collective-permute-start.1) | collective-permute-done | bytes 16416 | tf_op jit(solution)/shard_map/ppermute | solution.py:17
  67.4 6.4 %collective-permute-done.2 = f32[2,16,128]{2,1,0:T(8,128)S(1)} collective-permute-done((f32[2,16,128]{2,1,0:T(8,128)S(1)}, f32[2,16,128]{2,1,0:T(8,128)S(1)}, u32[]{:S(2)}, u32[]{:S(2)}) %collective-permute-start.2) | collective-permute-done | bytes 16416 | tf_op jit(solution)/shard_map/ppermute | solution.py:17
  73.8 6.5 %collective-permute-done.3 = f32[2,16,128]{2,1,0:T(8,128)S(1)} collective-permute-done((f32[2,16,128]{2,1,0:T(8,128)S(1)}, f32[2,16,128]{2,1,0:T(8,128)S(1)}, u32[]{:S(2)}, u32[]{:S(2)}) %collective-permute-start.3) | collective-permute-done | bytes 16416 | tf_op jit(solution)/shard_map/ppermute | solution.py:17
  80.3 6.4 %collective-permute-done.4 = f32[2,16,128]{2,1,0:T(8,128)S(1)} collective-permute-done((f32[2,16,128]{2,1,0:T(8,128)S(1)}, f32[2,16,128]{2,1,0:T(8,128)S(1)}, u32[]{:S(2)}, u32[]{:S(2)}) %collective-permute-start.4) | collective-permute-done | bytes 16416 | tf_op jit(solution)/shard_map/ppermute | solution.py:17
  86.8 6.4 %collective-permute-done.5 = f32[2,16,128]{2,1,0:T(8,128)S(1)} collective-permute-done((f32[2,16,128]{2,1,0:T(8,128)S(1)}, f32[2,16,128]{2,1,0:T(8,128)S(1)}, u32[]{:S(2)}, u32[]{:S(2)}) %collective-permute-start.5) | collective-permute-done | bytes 16416 | tf_op jit(solution)/shard_map/ppermute | solution.py:17
  93.2 6.4 %collective-permute-done.6 = f32[2,16,128]{2,1,0:T(8,128)S(1)} collective-permute-done((f32[2,16,128]{2,1,0:T(8,128)S(1)}, f32[2,16,128]{2,1,0:T(8,128)S(1)}, u32[]{:S(2)}, u32[]{:S(2)}) %collective-permute-start.6) | collective-permute-done | bytes 16416 | tf_op jit(solution)/shard_map/ppermute | solution.py:17
  99.6 0.6 gather_fusion
  100.2 8.1 %fusion.2 = f32[58,16,128]{2,1,0:T(8,128)S(1)} fusion(f32[58,16,128]{2,1,0:T(8,128)S(1)} %gather_fusion, f32[1,1,58,128,128]{4,3,2,1,0:T(8,128)} %param.9), kind=kOutput, calls=%fused_computation.4 | convolution fusion | flops 182452224 | bytes 4751360 | tf_op jit(solution)/shard_map/sij,skj->ski/dot_general | solution.py:55
  108.3 0.4 fusion.10
  108.7 0.6 copy.10
  109.4 17.7 %reduce-scatter.3.cloned.1.call-done = f32[2,16,128]{2,1,0:T(8,128)} async-done(((f32[8,16,128]{2,1,0:T(8,128)}), f32[2,16,128]{2,1,0:T(8,128)}) %reduce-scatter.3.cloned.1.call-update) | async-done | bytes 16400 | tf_op jit(solution)/shard_map/reduce_scatter | solution.py:64
  127.1 1.0 convolution_bitcast_fusion.1
  128.1 39.5 %psum.22 = f32[48,48]{0,1:T(8,128)S(1)} all-reduce(f32[48,48]{0,1:T(8,128)S(1)} %convolution_bitcast_fusion.1), channel_id=1, replica_groups=mesh['row'=8,'col'=4] {'row','col'}, use_global_device_ids=true, to_apply=%region_4.7 | all-reduce | flops 2304 | bytes 18432 | tf_op jit(solution)/shard_map/psum | solution.py:77
  167.8 0.2 subtract_subtract_fusion.1
  168.0 0.2 fusion.52
  168.4 0.2 fusion.30
  168.8 0.2 convolution_subtract_fusion.3
  169.8 1.5 cholesky.70
  171.3 0.6 compare_reduce_fusion.1
  172.0 0.6 fusion.94
  172.6 1.2 custom-call.8
  174.1 0.9 fusion.7
  175.3 2.3 collective-permute-start.7
  177.6 4.1 %collective-permute-done.7 = f32[2,16,128]{2,1,0:T(8,128)S(1)} collective-permute-done((f32[2,16,128]{2,1,0:T(8,128)S(1)}, f32[2,16,128]{2,1,0:T(8,128)S(1)}, u32[]{:S(2)}, u32[]{:S(2)}) %collective-permute-start.7) | collective-permute-done | bytes 16416 | tf_op jit(solution)/shard_map/ppermute | solution.py:17
  181.8 6.4 %collective-permute-done.8 = f32[2,16,128]{2,1,0:T(8,128)S(1)} collective-permute-done((f32[2,16,128]{2,1,0:T(8,128)S(1)}, f32[2,16,128]{2,1,0:T(8,128)S(1)}, u32[]{:S(2)}, u32[]{:S(2)}) %collective-permute-start.8) | collective-permute-done | bytes 16416 | tf_op jit(solution)/shard_map/ppermute | solution.py:17
  188.2 6.4 %collective-permute-done.9 = f32[2,16,128]{2,1,0:T(8,128)S(1)} collective-permute-done((f32[2,16,128]{2,1,0:T(8,128)S(1)}, f32[2,16,128]{2,1,0:T(8,128)S(1)}, u32[]{:S(2)}, u32[]{:S(2)}) %collective-permute-start.9) | collective-permute-done | bytes 16416 | tf_op jit(solution)/shard_map/ppermute | solution.py:17
  194.6 6.6 %collective-permute-done.10 = f32[2,16,128]{2,1,0:T(8,128)S(1)} collective-permute-done((f32[2,16,128]{2,1,0:T(8,128)S(1)}, f32[2,16,128]{2,1,0:T(8,128)S(1)}, u32[]{:S(2)}, u32[]{:S(2)}) %collective-permute-start.10) | collective-permute-done | bytes 16416 | tf_op jit(solution)/shard_map/ppermute | solution.py:17
  201.2 6.4 %collective-permute-done.11 = f32[2,16,128]{2,1,0:T(8,128)S(1)} collective-permute-done((f32[2,16,128]{2,1,0:T(8,128)S(1)}, f32[2,16,128]{2,1,0:T(8,128)S(1)}, u32[]{:S(2)}, u32[]{:S(2)}) %collective-permute-start.11) | collective-permute-done | bytes 16416 | tf_op jit(solution)/shard_map/ppermute | solution.py:17
  207.6 6.4 %collective-permute-done.12 = f32[2,16,128]{2,1,0:T(8,128)S(1)} collective-permute-done((f32[2,16,128]{2,1,0:T(8,128)S(1)}, f32[2,16,128]{2,1,0:T(8,128)S(1)}, u32[]{:S(2)}, u32[]{:S(2)}) %collective-permute-start.12) | collective-permute-done | bytes 16416 | tf_op jit(solution)/shard_map/ppermute | solution.py:17
  214.1 6.4 %collective-permute-done.13 = f32[2,16,128]{2,1,0:T(8,128)S(1)} collective-permute-done((f32[2,16,128]{2,1,0:T(8,128)S(1)}, f32[2,16,128]{2,1,0:T(8,128)S(1)}, u32[]{:S(2)}, u32[]{:S(2)}) %collective-permute-start.13) | collective-permute-done | bytes 16416 | tf_op jit(solution)/shard_map/ppermute | solution.py:17
  220.5 0.6 gather_fusion.1
  221.1 8.1 %fusion = f32[58,16,128]{2,1,0:T(8,128)S(1)} fusion(f32[58,16,128]{2,1,0:T(8,128)S(1)} %gather_fusion.1, f32[1,1,58,128,128]{4,3,2,1,0:T(8,128)} %param.9), kind=kOutput, calls=%fused_computation.2 | convolution fusion | flops 182452224 | bytes 4751360 | tf_op jit(solution)/shard_map/sij,skj->ski/dot_general | solution.py:55
  229.2 0.4 fusion.8
  229.6 0.6 copy.21
  230.3 17.6 %reduce-scatter.5.cloned.1.call-done = f32[2,16,128]{2,1,0:T(8,128)} async-done(((f32[8,16,128]{2,1,0:T(8,128)}), f32[2,16,128]{2,1,0:T(8,128)}) %reduce-scatter.5.cloned.1.call-update) | async-done | bytes 16400 | tf_op jit(solution)/shard_map/reduce_scatter | solution.py:64
  248.0 1.0 convolution_bitcast_fusion
  248.9 39.5 %psum.23 = f32[48,48]{0,1:T(8,128)S(1)} all-reduce(f32[48,48]{0,1:T(8,128)S(1)} %convolution_bitcast_fusion), channel_id=1, replica_groups=mesh['row'=8,'col'=4] {'row','col'}, use_global_device_ids=true, to_apply=%region_6.9 | all-reduce | flops 2304 | bytes 18432 | tf_op jit(solution)/shard_map/psum | solution.py:77
  288.5 0.8 fusion.26
  289.3 0.9 fusion.44
  290.2 0.2 fusion.28
  290.4 0.2 subtract_subtract_fusion
  290.6 0.2 fusion.46
  290.9 0.9 fusion.5
  291.8 0.8 fusion.4
  292.9 0.9 convolution_subtract_fusion.1
  293.7 0.9 convolution_subtract_fusion
  294.6 0.9 convolution_add_fusion.2
  295.6 0.9 convolution_add_fusion
  296.6 1.5 cholesky.81
  298.1 0.6 compare_reduce_fusion
  298.7 0.6 select_bitcast_fusion
  299.4 1.2 custom-call.9
  300.8 0.7 copy.33
  301.5 0.7 copy.32
  302.2 0.7 convolution_bitcast_fusion.2
  (70 shorter events, 3.6 us)
Async XLA Ops:
  7.2 0.7 copy-start
  7.2 101.1 %copy-start.1 = (s32[1,1,58]{2,1,0:T(1,128)S(1)}, s32[1,1,58]{2,1,0:T(1,128)}, u32[]{:S(2)}) copy-start(s32[1,1,58]{2,1,0:T(1,128)} %param.10) | copy-start | bytes 700
  7.2 119.9 %reduce-scatter.3.cloned.1.call-start = ((), (), s32[]{:S(2)}) async-start(), calls=%async_computation.2 | async-start | bytes 81920 | tf_op jit(solution)/shard_map/reduce_scatter | solution.py:64
  54.5 6.5 %collective-permute-start = (f32[2,16,128]{2,1,0:T(8,128)S(1)}, f32[2,16,128]{2,1,0:T(8,128)S(1)}, u32[]{:S(2)}, u32[]{:S(2)}) collective-permute-start(f32[2,16,128]{2,1,0:T(8,128)S(1)} %get-tuple-element.13), channel_id=1, source_target_pairs={{0,4},{4,8},{8,12},{12,16},{16,20},{20,24},{24,28},{28,0},{1,5},{5... | collective-permute-start | bytes 49160 | tf_op jit(solution)/shard_map/ppermute | solution.py:17
  60.9 6.4 %collective-permute-start.1 = (f32[2,16,128]{2,1,0:T(8,128)S(1)}, f32[2,16,128]{2,1,0:T(8,128)S(1)}, u32[]{:S(2)}, u32[]{:S(2)}) collective-permute-start(f32[2,16,128]{2,1,0:T(8,128)S(1)} %collective-permute-done), channel_id=1, source_target_pairs={{0,4},{4,8},{8,12},{12,16},{16,20},{20,24},{24,28},{28,0},{1,5},{5... | collective-permute-start | bytes 49160 | tf_op jit(solution)/shard_map/ppermute | solution.py:17
  67.4 6.4 %collective-permute-start.2 = (f32[2,16,128]{2,1,0:T(8,128)S(1)}, f32[2,16,128]{2,1,0:T(8,128)S(1)}, u32[]{:S(2)}, u32[]{:S(2)}) collective-permute-start(f32[2,16,128]{2,1,0:T(8,128)S(1)} %collective-permute-done.1), channel_id=1, source_target_pairs={{0,4},{4,8},{8,12},{12,16},{16,20},{20,24},{24,28},{28,0},{1,5},{5... | collective-permute-start | bytes 49160 | tf_op jit(solution)/shard_map/ppermute | solution.py:17
  73.8 6.5 %collective-permute-start.3 = (f32[2,16,128]{2,1,0:T(8,128)S(1)}, f32[2,16,128]{2,1,0:T(8,128)S(1)}, u32[]{:S(2)}, u32[]{:S(2)}) collective-permute-start(f32[2,16,128]{2,1,0:T(8,128)S(1)} %collective-permute-done.2), channel_id=1, source_target_pairs={{0,4},{4,8},{8,12},{12,16},{16,20},{20,24},{24,28},{28,0},{1,5},{5... | collective-permute-start | bytes 49160 | tf_op jit(solution)/shard_map/ppermute | solution.py:17
  80.3 6.4 %collective-permute-start.4 = (f32[2,16,128]{2,1,0:T(8,128)S(1)}, f32[2,16,128]{2,1,0:T(8,128)S(1)}, u32[]{:S(2)}, u32[]{:S(2)}) collective-permute-start(f32[2,16,128]{2,1,0:T(8,128)S(1)} %collective-permute-done.3), channel_id=1, source_target_pairs={{0,4},{4,8},{8,12},{12,16},{16,20},{20,24},{24,28},{28,0},{1,5},{5... | collective-permute-start | bytes 49160 | tf_op jit(solution)/shard_map/ppermute | solution.py:17
  86.7 6.4 %collective-permute-start.5 = (f32[2,16,128]{2,1,0:T(8,128)S(1)}, f32[2,16,128]{2,1,0:T(8,128)S(1)}, u32[]{:S(2)}, u32[]{:S(2)}) collective-permute-start(f32[2,16,128]{2,1,0:T(8,128)S(1)} %collective-permute-done.4), channel_id=1, source_target_pairs={{0,4},{4,8},{8,12},{12,16},{16,20},{20,24},{24,28},{28,0},{1,5},{5... | collective-permute-start | bytes 49160 | tf_op jit(solution)/shard_map/ppermute | solution.py:17
  93.2 6.4 %collective-permute-start.6 = (f32[2,16,128]{2,1,0:T(8,128)S(1)}, f32[2,16,128]{2,1,0:T(8,128)S(1)}, u32[]{:S(2)}, u32[]{:S(2)}) collective-permute-start(f32[2,16,128]{2,1,0:T(8,128)S(1)} %collective-permute-done.5), channel_id=1, source_target_pairs={{0,4},{4,8},{8,12},{12,16},{16,20},{20,24},{24,28},{28,0},{1,5},{5... | collective-permute-start | bytes 49160 | tf_op jit(solution)/shard_map/ppermute | solution.py:17
  109.4 138.6 %reduce-scatter.5.cloned.1.call-start = ((), (), s32[]{:S(2)}) async-start(), calls=%async_computation.3 | async-start | bytes 81920 | tf_op jit(solution)/shard_map/reduce_scatter | solution.py:64
  175.3 6.5 %collective-permute-start.7 = (f32[2,16,128]{2,1,0:T(8,128)S(1)}, f32[2,16,128]{2,1,0:T(8,128)S(1)}, u32[]{:S(2)}, u32[]{:S(2)}) collective-permute-start(f32[2,16,128]{2,1,0:T(8,128)S(1)} %get-tuple-element.15), channel_id=1, source_target_pairs={{0,4},{4,8},{8,12},{12,16},{16,20},{20,24},{24,28},{28,0},{1,5},{5... | collective-permute-start | bytes 49160 | tf_op jit(solution)/shard_map/ppermute | solution.py:17
  181.7 6.4 %collective-permute-start.8 = (f32[2,16,128]{2,1,0:T(8,128)S(1)}, f32[2,16,128]{2,1,0:T(8,128)S(1)}, u32[]{:S(2)}, u32[]{:S(2)}) collective-permute-start(f32[2,16,128]{2,1,0:T(8,128)S(1)} %collective-permute-done.7), channel_id=1, source_target_pairs={{0,4},{4,8},{8,12},{12,16},{16,20},{20,24},{24,28},{28,0},{1,5},{5... | collective-permute-start | bytes 49160 | tf_op jit(solution)/shard_map/ppermute | solution.py:17
  188.2 6.4 %collective-permute-start.9 = (f32[2,16,128]{2,1,0:T(8,128)S(1)}, f32[2,16,128]{2,1,0:T(8,128)S(1)}, u32[]{:S(2)}, u32[]{:S(2)}) collective-permute-start(f32[2,16,128]{2,1,0:T(8,128)S(1)} %collective-permute-done.8), channel_id=1, source_target_pairs={{0,4},{4,8},{8,12},{12,16},{16,20},{20,24},{24,28},{28,0},{1,5},{5... | collective-permute-start | bytes 49160 | tf_op jit(solution)/shard_map/ppermute | solution.py:17
  194.6 6.6 %collective-permute-start.10 = (f32[2,16,128]{2,1,0:T(8,128)S(1)}, f32[2,16,128]{2,1,0:T(8,128)S(1)}, u32[]{:S(2)}, u32[]{:S(2)}) collective-permute-start(f32[2,16,128]{2,1,0:T(8,128)S(1)} %collective-permute-done.9), channel_id=1, source_target_pairs={{0,4},{4,8},{8,12},{12,16},{16,20},{20,24},{24,28},{28,0},{1,5},{5... | collective-permute-start | bytes 49160 | tf_op jit(solution)/shard_map/ppermute | solution.py:17
  201.2 6.4 %collective-permute-start.11 = (f32[2,16,128]{2,1,0:T(8,128)S(1)}, f32[2,16,128]{2,1,0:T(8,128)S(1)}, u32[]{:S(2)}, u32[]{:S(2)}) collective-permute-start(f32[2,16,128]{2,1,0:T(8,128)S(1)} %collective-permute-done.10), channel_id=1, source_target_pairs={{0,4},{4,8},{8,12},{12,16},{16,20},{20,24},{24,28},{28,0},{1,5},{5... | collective-permute-start | bytes 49160 | tf_op jit(solution)/shard_map/ppermute | solution.py:17
  207.6 6.4 %collective-permute-start.12 = (f32[2,16,128]{2,1,0:T(8,128)S(1)}, f32[2,16,128]{2,1,0:T(8,128)S(1)}, u32[]{:S(2)}, u32[]{:S(2)}) collective-permute-start(f32[2,16,128]{2,1,0:T(8,128)S(1)} %collective-permute-done.11), channel_id=1, source_target_pairs={{0,4},{4,8},{8,12},{12,16},{16,20},{20,24},{24,28},{28,0},{1,5},{5... | collective-permute-start | bytes 49160 | tf_op jit(solution)/shard_map/ppermute | solution.py:17
  214.1 6.4 %collective-permute-start.13 = (f32[2,16,128]{2,1,0:T(8,128)S(1)}, f32[2,16,128]{2,1,0:T(8,128)S(1)}, u32[]{:S(2)}, u32[]{:S(2)}) collective-permute-start(f32[2,16,128]{2,1,0:T(8,128)S(1)} %collective-permute-done.12), channel_id=1, source_target_pairs={{0,4},{4,8},{8,12},{12,16},{16,20},{20,24},{24,28},{28,0},{1,5},{5... | collective-permute-start | bytes 49160 | tf_op jit(solution)/shard_map/ppermute | solution.py:17
Sparse Core Ops, SparseCore 0:
  109.5 17.5 reduce-scatter.2
  230.4 17.5 reduce-scatter.4
